TPU v7x, 256 devices: a whole 4x4x8 slice. The times are simulated.
256 devices in a mesh: grp: 8 (over x, z_lo), dev: 32 (over y, z_hi, core).
Axes of the slice: x: 4, y: 4, z: 8 (z_hi: 4, z_lo: 2; z = z_hi * 2 + z_lo), core: 2. Of those that a mesh axis runs over, the one named last changes fastest.
Arguments:
- query: bfloat16 [512, 128, 4096], P(('grp', 'dev')), may hold values from -100 to 100
- grad_out: bfloat16 [512, 128, 4096], P(('grp', 'dev')), may hold values from -6 to 6
- branch_kv: bfloat16 [512, 128, 1024], P(('grp', 'dev')), may hold values from -6 to 6
- root_kv: bfloat16 [1024, 1024], P('dev'), may hold values from -24 to 24
- lengths: int32 [512], P(('grp', 'dev')), may hold values from 0 to 128, as said below
- segments: int32 [512], P(('grp', 'dev')), may hold values from 0 to 3
Outputs:
- query_grad: bfloat16 [512, 128, 4096], P(('grp', 'dev'))
- branch_grad: bfloat16 [512, 128, 1024], P(('grp', 'dev'))
- root_grad: float32 [1024, 1024], P('dev')
Inputs may be any that keep to these rules, and one draw needn't show every extreme that they name: `lengths`: A slot with length 0 holds no branch. A device's slots with live positions come before its empty slots. Within a group, device d and device d + 32/2 (d < 16) hold exactly 2 slots with live positions together; a quarter of a group's devices hold 2 such slots and a quarter hold none.
All inputs are finite; a program needn't handle non-finite values.
Results may differ from a plain program's by a relative error of at most 0.0069.
Values may be sent and summed in bfloat16 or wider, within the bound.
A program may use at most 128 MiB of HBM per device.

v0:
```python
import jax
import jax.numpy as jnp
from jax import lax
from jax.sharding import PartitionSpec as P

H = 32
KVH = 4
DH = 128
SEGS = 4


def passed_along(block, axis, distance):
    devices = range(lax.axis_size(axis))
    route = [((i - distance) % len(devices), i) for i in devices]
    return lax.ppermute(block, axis, route)


def cut_along(x, dim, peers):
    dims = x.shape
    blocks = x.reshape(*dims[:dim], peers, dims[dim] // peers, *dims[dim + 1 :])
    return jnp.moveaxis(blocks, dim, 0)


def summed_on_arrival(x, axis, dim):
    blocks = cut_along(x, dim, lax.axis_size(axis))
    arrived = lax.all_to_all(blocks, axis, split_axis=0, concat_axis=0, tiled=True)
    return arrived.astype(jnp.float32).sum(axis=0)


def from_everyone(x, axis):
    copies = jnp.broadcast_to(x, (lax.axis_size(axis), *x.shape))
    return lax.all_to_all(copies, axis, split_axis=0, concat_axis=0, tiled=True)


def over_copies(x, axis):
    return from_everyone(x, axis).sum(axis=0)


def tile_grads(query, grad, branch, length, segment, root_keys):
    rows = query.shape[0]
    width = KVH * DH
    groups = H // KVH
    roots = root_keys.shape[0]
    everything = jnp.concatenate([root_keys, branch], axis=0)
    span = roots + rows
    scale = DH ** (-0.5)
    row_pos = lax.broadcasted_iota(jnp.int32, (rows, span), 0)
    col_pos = lax.broadcasted_iota(jnp.int32, (rows, span), 1)
    visible = jnp.where(
        col_pos < roots, col_pos < (segment + 1) * (roots // SEGS), col_pos - roots <= row_pos
    )
    live = lax.broadcasted_iota(jnp.int32, (rows, 1), 0) < length
    grad = jnp.where(live, grad, jnp.zeros_like(grad))
    dq_parts = []
    dk_parts = []
    dv_parts = []
    for head in range(KVH):
        q_head = query[:, head * groups * DH : (head + 1) * groups * DH].reshape(rows, groups, DH)
        g_head = grad[:, head * groups * DH : (head + 1) * groups * DH].reshape(rows, groups, DH)
        k_head = everything[:, head * DH : (head + 1) * DH]
        v_head = everything[:, width + head * DH : width + (head + 1) * DH]
        scores = (
            jnp.einsum("tgd,ld->gtl", q_head, k_head, preferred_element_type=jnp.float32) * scale
        )
        scores = jnp.where(visible[None], scores, jnp.float32(-1e30))
        peak = jnp.max(scores, axis=-1, keepdims=True)
        weights = jnp.exp(scores - peak)
        weights = weights / jnp.sum(weights, axis=-1, keepdims=True)
        probs = weights.astype(jnp.bfloat16)
        output = jnp.einsum("gtl,ld->tgd", probs, v_head, preferred_element_type=jnp.float32)
        delta = jnp.sum(g_head.astype(jnp.float32) * output, axis=-1)
        dv_parts.append(
            jnp.einsum("gtl,tgd->ld", probs, g_head, preferred_element_type=jnp.float32)
        )
        prob_grad = jnp.einsum("tgd,ld->gtl", g_head, v_head, preferred_element_type=jnp.float32)
        score_grad = (weights * (prob_grad - delta.T[:, :, None]) * scale).astype(jnp.bfloat16)
        dq_parts.append(
            jnp.einsum(
                "gtl,ld->tgd", score_grad, k_head, preferred_element_type=jnp.float32
            ).reshape(rows, groups * DH)
        )
        dk_parts.append(
            jnp.einsum("gtl,tgd->ld", score_grad, q_head, preferred_element_type=jnp.float32)
        )
    dq = jnp.concatenate(dq_parts, axis=1).astype(jnp.bfloat16)
    dkv = jnp.concatenate(dk_parts + dv_parts, axis=1)
    return (dq, dkv[roots:].astype(jnp.bfloat16), dkv[:roots])


def local(query, grad_out, branch_kv, root_kv, lengths, segments):
    root_keys = lax.all_gather(root_kv, "dev", axis=0, tiled=True)
    half = lax.axis_size("dev") // 2
    live_count = jnp.sum((lengths > 0).astype(jnp.int32))
    arrived = passed_along(
        (query[1], grad_out[1], branch_kv[1], lengths[1:], segments[1:]), "dev", half
    )
    resident = live_count > 0
    q_tile = jnp.where(resident, query[0], arrived[0])
    g_tile = jnp.where(resident, grad_out[0], arrived[1])
    b_tile = jnp.where(resident, branch_kv[0], arrived[2])
    length = jnp.where(resident, lengths[0], arrived[3][0])
    segment = jnp.where(resident, segments[0], arrived[4][0])
    dq, dbranch, total = tile_grads(q_tile, g_tile, b_tile, length, segment, root_keys)
    returned = passed_along((dq, dbranch), "dev", half)
    second = live_count > 1
    query_grad = jnp.stack(
        [
            jnp.where(resident, dq, jnp.zeros_like(dq)),
            jnp.where(second, returned[0], jnp.zeros_like(dq)),
        ]
    )
    branch_grad = jnp.stack(
        [
            jnp.where(resident, dbranch, jnp.zeros_like(dbranch)),
            jnp.where(second, returned[1], jnp.zeros_like(dbranch)),
        ]
    )
    within = summed_on_arrival(total.astype(jnp.bfloat16), "dev", 0)
    root_grad = over_copies(within, "grp")
    return (query_grad, branch_grad, root_grad)


def solution(mesh):
    placed = (
        P(("grp", "dev"), None, None),
        P(("grp", "dev"), None, None),
        P(("grp", "dev"), None, None),
        P("dev", None),
        P(("grp", "dev")),
        P(("grp", "dev")),
    )
    return jax.shard_map(
        local,
        mesh=mesh,
        in_specs=placed,
        out_specs=(P(("grp", "dev"), None, None), P(("grp", "dev"), None, None), P("dev", None)),
        check_vma=False,
    )
```

profile of v0, /device:TPU:8, one launch (start us, length us, event | category | flops | bytes accessed | tf_op | source)
XLA Modules:
  0.0 251.1 jit_solution(15265945719861936562)
XLA Ops:
  8.2 2.4 collective-permute-start
  10.6 1.3 fusion.109
  11.9 1.2 collective-permute-start.1
  13.1 1.7 fusion.105
  14.8 1.3 copy.208
  16.2 2.3 collective-permute-start.2
  19.0 1.2 collective-permute-start.3
  20.3 1.7 fusion.106
  22.0 1.3 copy.210
  23.3 2.3 collective-permute-start.4
  29.4 1.2 fusion.45
  30.7 14.4 %collective-permute-done.3 = s32[1]{0:T(128)} collective-permute-done((s32[1]{0:T(128)}, s32[1]{0:T(128)}, u32[]{:S(2)}, u32[]{:S(2)}) %collective-permute-start.3) | collective-permute-done | bytes 36 | tf_op jit(solution)/shard_map/ppermute | solution.py:15
  46.4 1.0 bitcast_select_fusion.10
  48.5 17.4 %collective-permute-done.4 = bf16[128,4096]{0,1:T(8,128)(2,1)} collective-permute-done((bf16[128,4096]{0,1:T(8,128)(2,1)}, bf16[128,4096]{0,1:T(8,128)(2,1)}, u32[]{:S(2)}, u32[]{:S(2)}) %collective-permute-start.4) | collective-permute-done | bytes 1048608 | tf_op jit(solution)/shard_map/ppermute | solution.py:15
  67.7 29.8 %all-gather.2.cloned.1.call-done = bf16[1024,1024]{1,0:T(8,128)(2,1)} async-done(((bf16[32,1024]{1,0:T(8,128)(2,1)}), bf16[1024,1024]{1,0:T(8,128)(2,1)}) %all-gather.2.cloned.1.call-update) | async-done | bytes 2097168 | tf_op jit(solution)/shard_map/all_gather | solution.py:91
  97.5 2.3 fusion.47
  99.8 4.4 %exponential_reduce_fusion.3 = (f32[8,128]{1,0:T(8,128)}, f32[8,128,1152]{1,2,0:T(8,128)}) fusion(pred[128,1152]{0,1:T(8,128)(4,1)S(1)} %fusion.45, bf16[128,8,128]{0,2,1:T(8,128)(2,1)S(1)} %bitcast.302, bf16[1152,128]{1,0:T(8,128)(2,1)S(1)} %get-tuple-element.11), kind=kOutput, calls=%fused_computation.50 | convolution fusion | flops 306709632 | bytes 5427200 | tf_op jit(solution)/shard_map/sub | solution.py:67
  104.2 3.1 %fusion.40 = bf16[8,128,1152]{1,2,0:T(8,128)(2,1)S(1)} fusion(f32[8,128]{1,0:T(8,128)} %get-tuple-element.38, f32[8,128,1152]{1,2,0:T(8,128)} %get-tuple-element.39), kind=kLoop, calls=%fused_computation.77 | loop fusion | flops 2359296 | bytes 7081984 | tf_op jit(solution)/shard_map/convert_element_type | solution.py:69
  107.9 1.8 copy-done.20
  109.7 1.3 fusion.19
  111.0 1.6 fusion.31
  112.6 5.4 %exponential_reduce_fusion.2 = (f32[8,128]{1,0:T(8,128)}, f32[8,128,1152]{1,2,0:T(8,128)}) fusion(pred[128,1152]{0,1:T(8,128)(4,1)S(1)} %fusion.45, bf16[128,8,128]{0,2,1:T(8,128)(2,1)} %bitcast.300, bf16[1152,128]{1,0:T(8,128)(2,1)} %get-tuple-element.12), kind=kOutput, calls=%fused_computation.48 | convolution fusion | flops 306709632 | bytes 5427200 | tf_op jit(solution)/shard_map/sub | solution.py:67
  118.0 3.1 %fusion.41 = bf16[8,128,1152]{1,2,0:T(8,128)(2,1)S(1)} fusion(f32[8,128]{1,0:T(8,128)} %get-tuple-element.36, f32[8,128,1152]{1,2,0:T(8,128)} %get-tuple-element.37), kind=kLoop, calls=%fused_computation.78 | loop fusion | flops 2359296 | bytes 7081984 | tf_op jit(solution)/shard_map/convert_element_type | solution.py:69
  122.6 1.7 copy-done.21
  124.4 1.3 fusion.16
  125.7 1.5 fusion.30
  127.3 5.4 %exponential_reduce_fusion.1 = (f32[8,128]{1,0:T(8,128)}, f32[8,128,1152]{1,2,0:T(8,128)}) fusion(pred[128,1152]{0,1:T(8,128)(4,1)S(1)} %fusion.45, bf16[128,8,128]{0,2,1:T(8,128)(2,1)} %bitcast.298, bf16[1152,128]{1,0:T(8,128)(2,1)} %get-tuple-element.13), kind=kOutput, calls=%fused_computation.46 | convolution fusion | flops 306709632 | bytes 5427200 | tf_op jit(solution)/shard_map/sub | solution.py:67
  132.7 3.3 %fusion.42 = bf16[8,128,1152]{1,2,0:T(8,128)(2,1)S(1)} fusion(f32[8,128]{1,0:T(8,128)} %get-tuple-element.34, f32[8,128,1152]{1,2,0:T(8,128)} %get-tuple-element.35), kind=kLoop, calls=%fused_computation.79 | loop fusion | flops 2359296 | bytes 7081984 | tf_op jit(solution)/shard_map/convert_element_type | solution.py:69
  137.4 1.8 copy-done.19
  139.2 1.3 fusion.13
  140.6 1.6 fusion.29
  142.2 5.3 %exponential_reduce_fusion = (f32[8,128]{1,0:T(8,128)}, f32[8,128,1152]{1,2,0:T(8,128)}) fusion(pred[128,1152]{0,1:T(8,128)(4,1)S(1)} %fusion.45, bf16[128,8,128]{0,2,1:T(8,128)(2,1)S(1)} %bitcast.296, bf16[1152,128]{1,0:T(8,128)(2,1)} %get-tuple-element.15), kind=kOutput, calls=%fused_computation.44 | convolution fusion | flops 306709632 | bytes 5427200 | tf_op jit(solution)/shard_map/sub | solution.py:67
  147.5 3.1 %fusion.43 = bf16[8,128,1152]{1,2,0:T(8,128)(2,1)S(1)} fusion(f32[8,128]{1,0:T(8,128)} %get-tuple-element.32, f32[8,128,1152]{1,2,0:T(8,128)} %get-tuple-element.33), kind=kLoop, calls=%fused_computation.80 | loop fusion | flops 2359296 | bytes 7081984 | tf_op jit(solution)/shard_map/convert_element_type | solution.py:69
  150.7 1.5 multiply_reduce_fusion
  152.3 1.3 fusion.10
  160.5 1.6 slice.137
  162.6 7.3 %all-to-all-start = ((bf16[32,32,1024]{2,1,0:T(8,128)(2,1)}), bf16[32,32,1024]{2,1,0:T(8,128)(2,1)}, u32[]{:S(2)}, u32[]{:S(2)}) async-start(bf16[32,32,1024]{2,1,0:T(8,128)(2,1)} %bitcast.275), calls=%async_computation | async-start | bytes 4194304 | tf_op jit(solution)/shard_map/all_to_all | solution.py:26
  170.6 1.9 select_bitcast_fusion.2
  172.5 2.1 collective-permute-start.6
  174.6 1.5 convolution_convert_fusion.3
  178.4 1.1 pad_maximum_fusion.1
  179.5 1.4 collective-permute-start.5
  180.9 38.8 %all-to-all-done = bf16[32,32,1024]{2,1,0:T(8,128)(2,1)} async-done(((bf16[32,32,1024]{2,1,0:T(8,128)(2,1)}), bf16[32,32,1024]{2,1,0:T(8,128)(2,1)}, u32[]{:S(2)}, u32[]{:S(2)}) %all-to-all-start) | async-done | bytes 2097184 | tf_op jit(solution)/shard_map/all_to_all | solution.py:26
  219.7 2.0 convert_reduce_fusion
  221.6 1.1 broadcast_in_dim.54
  222.7 4.3 %all-to-all-start.1 = ((f32[8,32,1024]{2,1,0:T(8,128)}), f32[8,32,1024]{2,1,0:T(8,128)S(1)}, u32[]{:S(2)}, u32[]{:S(2)}) async-start(f32[8,32,1024]{2,1,0:T(8,128)} %broadcast_in_dim.54), calls=%async_computation.1 | async-start | bytes 2097152 | tf_op jit(solution)/shard_map/all_to_all | solution.py:32
  229.0 2.7 %copy.150 = bf16[2,128,4096]{2,1,0:T(8,128)(2,1)} copy(bf16[2,128,4096]{1,2,0:T(8,128)(2,1)S(1)} %pad_maximum_fusion) | data formatting | bytes 4194304
  231.8 11.7 %all-to-all-done.1 = f32[8,32,1024]{2,1,0:T(8,128)S(1)} async-done(((f32[8,32,1024]{2,1,0:T(8,128)}), f32[8,32,1024]{2,1,0:T(8,128)S(1)}, u32[]{:S(2)}, u32[]{:S(2)}) %all-to-all-start.1) | async-done | bytes 1048608 | tf_op jit(solution)/shard_map/all_to_all | solution.py:32
  (113 shorter events, 22.2 us)
Async XLA Ops:
  7.2 90.3 %all-gather.2.cloned.1.call-start = ((), (), s32[]{:S(2)}) async-start(), calls=%async_computation.2 | async-start | bytes 2162688 | tf_op jit(solution)/shard_map/all_gather | solution.py:91
  8.2 38.2 %collective-permute-start = (bf16[128,1024]{1,0:T(8,128)(2,1)S(1)}, bf16[128,1024]{1,0:T(8,128)(2,1)}, u32[]{:S(2)}, u32[]{:S(2)}) collective-permute-start(bf16[128,1024]{1,0:T(8,128)(2,1)S(1)} %slice_bitcast_fusion), channel_id=1, source_target_pairs={{16,0},{17,1},{18,2},{19,3},{20,4},{21,5},{22,6},{23,7},{24,8},{25... | collective-permute-start | bytes 786440 | tf_op jit(solution)/shard_map/ppermute | solution.py:15
  11.9 6.5 %copy-start.39 = (s32[2]{0:T(128)S(1)}, s32[2]{0:T(128)}, u32[]{:S(2)}) copy-start(s32[2]{0:T(128)} %param.10) | copy-start | bytes 28
  11.9 16.3 %collective-permute-start.1 = (s32[1]{0:T(128)}, s32[1]{0:T(128)}, u32[]{:S(2)}, u32[]{:S(2)}) collective-permute-start(s32[1]{0:T(128)} %get-tuple-element.28), channel_id=1, source_target_pairs={{16,0},{17,1},{18,2},{19,3},{20,4},{21,5},{22,6},{23,7},{24,8},{25... | collective-permute-start | bytes 20 | tf_op jit(solution)/shard_map/ppermute | solution.py:15
  16.2 31.3 %collective-permute-start.2 = (bf16[128,4096]{0,1:T(8,128)(2,1)}, bf16[128,4096]{0,1:T(8,128)(2,1)}, u32[]{:S(2)}, u32[]{:S(2)}) collective-permute-start(bf16[128,4096]{0,1:T(8,128)(2,1)} %bitcast.7), channel_id=1, source_target_pairs={{16,0},{17,1},{18,2},{19,3},{20,4},{21,5},{22,6},{23,7},{24,8},{25... | collective-permute-start | bytes 3145736 | tf_op jit(solution)/shard_map/ppermute | solution.py:15
  19.0 26.0 %collective-permute-start.3 = (s32[1]{0:T(128)}, s32[1]{0:T(128)}, u32[]{:S(2)}, u32[]{:S(2)}) collective-permute-start(s32[1]{0:T(128)} %get-tuple-element.30), channel_id=1, source_target_pairs={{16,0},{17,1},{18,2},{19,3},{20,4},{21,5},{22,6},{23,7},{24,8},{25... | collective-permute-start | bytes 20 | tf_op jit(solution)/shard_map/ppermute | solution.py:15
  23.3 42.6 %collective-permute-start.4 = (bf16[128,4096]{0,1:T(8,128)(2,1)}, bf16[128,4096]{0,1:T(8,128)(2,1)}, u32[]{:S(2)}, u32[]{:S(2)}) collective-permute-start(bf16[128,4096]{0,1:T(8,128)(2,1)} %bitcast.293), channel_id=1, source_target_pairs={{16,0},{17,1},{18,2},{19,3},{20,4},{21,5},{22,6},{23,7},{24,8},{25... | collective-permute-start | bytes 3145736 | tf_op jit(solution)/shard_map/ppermute | solution.py:15
  48.5 51.3 %copy-start.33 = (bf16[128,1024]{0,1:T(8,128)(2,1)}, bf16[128,1024]{0,1:T(8,128)(2,1)S(1)}, u32[]{:S(2)}) copy-start(bf16[128,1024]{0,1:T(8,128)(2,1)S(1)} %get-tuple-element.20) | copy-start | bytes 786436
  99.8 4.4 %copy-start.25 = (bf16[1152,128]{1,0:T(8,128)(2,1)}, bf16[1152,128]{1,0:T(8,128)(2,1)S(1)}, u32[]{:S(2)}) copy-start(bf16[1152,128]{1,0:T(8,128)(2,1)S(1)} %get-tuple-element.11) | copy-start | bytes 884740
  104.2 3.1 %copy-start.4 = (bf16[1024,1024]{1,0:T(8,128)(2,1)S(1)}, bf16[1024,1024]{1,0:T(8,128)(2,1)}, u32[]{:S(2)}) copy-start(bf16[1024,1024]{1,0:T(8,128)(2,1)} %all-gather.2.cloned.1.call-done) | copy-start | bytes 6291460
  107.3 2.3 copy-start.20
  107.4 2.3 copy-start.37
  109.7 1.3 copy-start.34
  111.0 1.6 copy-start.7
  118.0 3.1 %copy-start.5 = (bf16[1024,1024]{1,0:T(8,128)(2,1)S(1)}, bf16[1024,1024]{1,0:T(8,128)(2,1)}, u32[]{:S(2)}) copy-start(bf16[1024,1024]{1,0:T(8,128)(2,1)} %all-gather.2.cloned.1.call-done) | copy-start | bytes 6291460
  121.2 1.5 copy-start
  121.2 3.2 %copy-start.21 = (f32[8,128,1152]{1,2,0:T(8,128)S(1)}, f32[8,128,1152]{1,2,0:T(8,128)}, u32[]{:S(2)}) copy-start(f32[8,128,1152]{1,2,0:T(8,128)} %get-tuple-element.37) | copy-start | bytes 14155780
  121.2 3.2 %copy-start.38 = (f32[8,128]{1,0:T(8,128)S(1)}, f32[8,128]{1,0:T(8,128)}, u32[]{:S(2)}) copy-start(f32[8,128]{1,0:T(8,128)} %get-tuple-element.36) | copy-start | bytes 12292
  124.4 1.3 copy-start.32
  125.7 1.5 copy-start.9
  132.7 3.4 %copy-start.6 = (bf16[1024,1024]{1,0:T(8,128)(2,1)S(1)}, bf16[1024,1024]{1,0:T(8,128)(2,1)}, u32[]{:S(2)}) copy-start(bf16[1024,1024]{1,0:T(8,128)(2,1)} %all-gather.2.cloned.1.call-done) | copy-start | bytes 6291460
  136.0 1.4 copy-start.2
  136.0 3.2 %copy-start.19 = (f32[8,128,1152]{1,2,0:T(8,128)S(1)}, f32[8,128,1152]{1,2,0:T(8,128)}, u32[]{:S(2)}) copy-start(f32[8,128,1152]{1,2,0:T(8,128)} %get-tuple-element.35) | copy-start | bytes 14155780
  136.0 3.2 %copy-start.36 = (f32[8,128]{1,0:T(8,128)S(1)}, f32[8,128]{1,0:T(8,128)}, u32[]{:S(2)}) copy-start(f32[8,128]{1,0:T(8,128)} %get-tuple-element.34) | copy-start | bytes 12292
  139.2 1.3 copy-start.31
  140.6 1.6 copy-start.11
  140.6 1.6 copy-start.29
  147.5 3.2 %copy-start.26 = (bf16[1152,128,1]{1,0,2:T(8,128)(2,1)S(1)}, bf16[1152,128,1]{1,0,2:T(8,128)(2,1)}, u32[]{:S(2)}) copy-start(bf16[1152,128,1]{1,0,2:T(8,128)(2,1)} %get-tuple-element.14) | copy-start | bytes 884740
  147.5 4.7 %copy-start.18 = (f32[8,128,1152]{1,2,0:T(8,128)S(1)}, f32[8,128,1152]{1,2,0:T(8,128)}, u32[]{:S(2)}) copy-start(f32[8,128,1152]{1,2,0:T(8,128)} %get-tuple-element.33) | copy-start | bytes 14155780
  150.6 1.6 copy-start.28
  150.6 1.6 copy-start.35
  152.2 1.7 copy-start.16
  152.2 1.7 copy-start.30
  153.9 1.4 copy-start.13
  155.4 1.7 copy-start.1
  157.0 1.7 copy-start.3
  160.5 2.1 copy-start.17
  162.6 12.0 %copy-start.8 = (bf16[8,128,1152]{1,2,0:T(8,128)(2,1)S(1)}, bf16[8,128,1152]{1,2,0:T(8,128)(2,1)}, u32[]{:S(2)}) copy-start(bf16[8,128,1152]{1,2,0:T(8,128)(2,1)} %copy-done.7) | copy-start | bytes 7077892
  162.6 57.0 %all-to-all-start = ((bf16[32,32,1024]{2,1,0:T(8,128)(2,1)}), bf16[32,32,1024]{2,1,0:T(8,128)(2,1)}, u32[]{:S(2)}, u32[]{:S(2)}) async-start(bf16[32,32,1024]{2,1,0:T(8,128)(2,1)} %bitcast.275), calls=%async_computation | async-start | bytes 4194304 | tf_op jit(solution)/shard_map/all_to_all | solution.py:26
  169.9 6.2 %copy-start.24 = (bf16[1152,128]{1,0:T(8,128)(2,1)S(1)}, bf16[1152,128]{1,0:T(8,128)(2,1)}, u32[]{:S(2)}) copy-start(bf16[1152,128]{1,0:T(8,128)(2,1)} %get-tuple-element.12) | copy-start | bytes 884740
  170.6 5.6 %copy-start.10 = (bf16[8,128,1152]{1,2,0:T(8,128)(2,1)S(1)}, bf16[8,128,1152]{1,2,0:T(8,128)(2,1)}, u32[]{:S(2)}) copy-start(bf16[8,128,1152]{1,2,0:T(8,128)(2,1)} %copy-done.9) | copy-start | bytes 7077892
  172.5 4.2 %copy-start.12 = (bf16[8,128,1152]{1,2,0:T(8,128)(2,1)S(1)}, bf16[8,128,1152]{1,2,0:T(8,128)(2,1)}, u32[]{:S(2)}) copy-start(bf16[8,128,1152]{1,2,0:T(8,128)(2,1)} %copy-done.11) | copy-start | bytes 7077892
  172.5 4.2 %copy-start.23 = (bf16[1152,128]{1,0:T(8,128)(2,1)S(1)}, bf16[1152,128]{1,0:T(8,128)(2,1)}, u32[]{:S(2)}) copy-start(bf16[1152,128]{1,0:T(8,128)(2,1)} %get-tuple-element.13) | copy-start | bytes 884740
  172.5 54.7 %collective-permute-start.6 = (bf16[128,1024]{1,0:T(8,128)(2,1)}, bf16[128,1024]{1,0:T(8,128)(2,1)}, u32[]{:S(2)}, u32[]{:S(2)}) collective-permute-start(bf16[128,1024]{1,0:T(8,128)(2,1)} %get-tuple-element.10), channel_id=1, source_target_pairs={{16,0},{17,1},{18,2},{19,3},{20,4},{21,5},{22,6},{23,7},{24,8},{25... | collective-permute-start | bytes 786440 | tf_op jit(solution)/shard_map/ppermute | solution.py:15
  176.2 1.7 copy-start.14
  176.2 1.7 copy-start.22
  179.5 49.3 %collective-permute-start.5 = (bf16[128,4096]{0,1:T(8,128)(2,1)}, bf16[128,4096]{0,1:T(8,128)(2,1)S(1)}, u32[]{:S(2)}, u32[]{:S(2)}) collective-permute-start(bf16[128,4096]{0,1:T(8,128)(2,1)} %pad_maximum_fusion.1), channel_id=1, source_target_pairs={{16,0},{17,1},{18,2},{19,3},{20,4},{21,5},{22,6},{23,7},{24,8},{25... | collective-permute-start | bytes 3145736 | tf_op jit(solution)/shard_map/ppermute | solution.py:15
  222.7 20.8 %all-to-all-start.1 = ((f32[8,32,1024]{2,1,0:T(8,128)}), f32[8,32,1024]{2,1,0:T(8,128)S(1)}, u32[]{:S(2)}, u32[]{:S(2)}) async-start(f32[8,32,1024]{2,1,0:T(8,128)} %broadcast_in_dim.54), calls=%async_computation.1 | async-start | bytes 2097152 | tf_op jit(solution)/shard_map/all_to_all | solution.py:32
  (2 other events, 1.9 us)
Sparse Core Ops, SparseCore 0:
  10.7 86.7 all-gather.1
where the time goes:
time: 252 us; the launch traced here: 251 us
  waiting for transfers between devices  112 us (44%)
  matrix products  41.3 us (16%)
  local copies, waits for them, and re-layouts  29.5 us (12%)
  other arithmetic  25.2 us (10%)
  starting transfers between devices  24.5 us (10%)
  between operations  18.5 us (7%)
    all_to_all x1, waiting for transfers between devices, summed_on_arrival(): lax.all_to_all(blocks, axis, split_axis=0, concat_axis=0, tiled=True)  38.8 us
    ppermute x7, waiting for transfers between devices, passed_along(): return lax.ppermute(block, axis, route)  31.7 us
    all_gather x1, waiting for transfers between devices, local(): root_keys = lax.all_gather(root_kv, 'dev', axis=0, tiled=True)  29.8 us
    sub x4, matrix products, tile_grads(): weights = jnp.exp(scores - peak)  20.5 us
    unnamed x85, local copies, waits for them, and re-layouts  18.8 us
    ppermute x7, starting transfers between devices, passed_along(): return lax.ppermute(block, axis, route)  13 us
    convert_element_type x4, other arithmetic, tile_grads(): probs = weights.astype(jnp.bfloat16)  12.7 us
    all_to_all x1, waiting for transfers between devices, from_everyone(): return lax.all_to_all(copies, axis, split_axis=0, concat_axis=0, tiled=True)  11.7 us
  transfers between devices with their start and end apart: 10, of which 5 were waited for; matrix products, arithmetic and copies ran while one was open for 11% of the time, Pallas kernels for 0%

commit v1 on v0

--- a/solution.py
+++ b/solution.py
@@ -1,3 +1,4 @@
+import functools
 import jax
 import jax.numpy as jnp
 from jax import lax
@@ -7,6 +8,15 @@
 KVH = 4
 DH = 128
 SEGS = 4
+
+
+def perform_slabs(panel, comm_axis):
+    carry = jnp.stack([panel for _ in range(jax.lax.axis_size(comm_axis))])
+    q_next = jax.lax.all_to_all(carry, axis_name=comm_axis, split_axis=0, concat_axis=0)
+    return jnp.concatenate(q_next, axis=0)
+
+
+outputs_raise = functools.partial(perform_slabs, comm_axis="dev")
 
 
 def passed_along(block, axis, distance):
@@ -88,7 +98,7 @@
 
 
 def local(query, grad_out, branch_kv, root_kv, lengths, segments):
-    root_keys = lax.all_gather(root_kv, "dev", axis=0, tiled=True)
+    root_keys = outputs_raise(root_kv)
     half = lax.axis_size("dev") // 2
     live_count = jnp.sum((lengths > 0).astype(jnp.int32))
     arrived = passed_along(

time: 252 us -> 256 us (1.016)
  starting transfers between devices: 24.5 us -> 39.4 us
  between operations: 18.5 us -> 4.9 us
  local copies, waits for them, and re-layouts: 29.5 us -> 42.6 us
  waiting for transfers between devices: 112 us -> 103 us
    all_gather x1 -> x0, waiting for transfers between devices: 29.8 us -> none  [local(): root_keys = lax.all_gather(root_kv, 'dev', axis=0, tiled=True)]
    ppermute x7, waiting for transfers between devices: 31.7 us -> 52.6 us  [passed_along(): return lax.ppermute(block, axis, route)]
    all_to_all x0 -> x1, starting transfers between devices: none -> 10.5 us  [perform_slabs(): jax.lax.all_to_all(carry, axis_name=comm_axis, split_axis=0, concat_axis=0)]
    unnamed x85 -> x111, local copies, waits for them, and re-layouts: 18.8 us -> 26.9 us
    all_to_all x1, starting transfers between devices: 7.26 us -> 11.5 us  [summed_on_arrival(): lax.all_to_all(blocks, axis, split_axis=0, concat_axis=0, tiled=True)]
  transfers between devices with their start and end apart: 10 -> 10, of which waited for: 5 -> 3; matrix products, arithmetic and copies ran while one was open for 11% -> 15% of each run, Pallas kernels for 0% -> 0%
where the time goes in v1:
time: 256 us; the launch traced here: 255 us
  waiting for transfers between devices  103 us (40%)
  local copies, waits for them, and re-layouts  42.6 us (17%)
  matrix products  40 us (16%)
  starting transfers between devices  39.4 us (15%)
  other arithmetic  25.3 us (10%)
  between operations  4.9 us (2%)
    ppermute x7, waiting for transfers between devices, passed_along(): return lax.ppermute(block, axis, route)  52.6 us
    all_to_all x1, waiting for transfers between devices, summed_on_arrival(): lax.all_to_all(blocks, axis, split_axis=0, concat_axis=0, tiled=True)  38.9 us
    unnamed x111, local copies, waits for them, and re-layouts  26.9 us
    sub x4, matrix products, tile_grads(): weights = jnp.exp(scores - peak)  20 us
    ppermute x7, starting transfers between devices, passed_along(): return lax.ppermute(block, axis, route)  13 us
    convert_element_type x4, other arithmetic, tile_grads(): probs = weights.astype(jnp.bfloat16)  12.4 us
    all_to_all x1, starting transfers between devices, summed_on_arrival(): lax.all_to_all(blocks, axis, split_axis=0, concat_axis=0, tiled=True)  11.5 us
    all_to_all x1, waiting for transfers between devices, from_everyone(): return lax.all_to_all(copies, axis, split_axis=0, concat_axis=0, tiled=True)  11.2 us
  transfers between devices with their start and end apart: 10, of which 3 were waited for; matrix products, arithmetic and copies ran while one was open for 15% of the time, Pallas kernels for 0%

profile of v1, /device:TPU:8, one launch (start us, length us, event | category | flops | bytes accessed | tf_op | source)
XLA Modules:
  0.0 254.9 jit_solution(5021201688280797955)
XLA Ops:
  0.6 1.3 fusion.110
  1.9 2.3 collective-permute-start.3
  4.2 2.4 stack.12
  6.7 10.5 %all-to-all-start = ((bf16[32,32,1024]{2,1,0:T(8,128)(2,1)}), bf16[32,32,1024]{2,1,0:T(8,128)(2,1)S(1)}, u32[]{:S(2)}, u32[]{:S(2)}) async-start(bf16[32,32,1024]{2,1,0:T(8,128)(2,1)} %stack.12), calls=%async_computation | async-start | bytes 4194304 | tf_op jit(solution)/shard_map/all_to_all | solution.py:15
  17.1 2.7 %fusion.105 = (bf16[1,128,4096]{2,1,0:T(8,128)(2,1)S(1)}, bf16[1,128,4096]{2,1,0:T(8,128)(2,1)}) fusion(bf16[2,128,4096]{2,1,0:T(8,128)(2,1)} %param.6), kind=kLoop, calls=%fused_computation.154 | loop fusion | bytes 4194304 | tf_op jit(solution)/shard_map/slice | solution.py:108
  19.9 2.3 copy.208
  22.1 2.1 collective-permute-start.2
  24.2 3.1 %fusion.106 = (bf16[1,128,4096]{2,1,0:T(8,128)(2,1)}, bf16[1,128,4096]{2,1,0:T(8,128)(2,1)}) fusion(bf16[2,128,4096]{2,1,0:T(8,128)(2,1)} %param.7), kind=kLoop, calls=%fused_computation.155 | loop fusion | bytes 4194304 | tf_op jit(solution)/shard_map/slice | solution.py:109
  27.3 2.3 copy.210
  29.6 1.4 collective-permute-start.4
  32.0 2.2 collective-permute-start
  34.7 1.4 collective-permute-start.1
  36.8 1.3 copy.207
  38.1 2.3 copy.209
  41.1 52.6 %collective-permute-done.1 = s32[1]{0:T(128)} collective-permute-done((s32[1]{0:T(128)}, s32[1]{0:T(128)}, u32[]{:S(2)}, u32[]{:S(2)}) %collective-permute-start.1) | collective-permute-done | bytes 36 | tf_op jit(solution)/shard_map/ppermute | solution.py:25
  94.8 1.2 fusion.45
  97.5 1.8 fusion.44
  101.2 1.2 fusion.47
  102.4 5.4 %exponential_reduce_fusion.3 = (f32[8,128]{1,0:T(8,128)}, f32[8,128,1152]{1,2,0:T(8,128)}) fusion(pred[128,1152]{0,1:T(8,128)(4,1)S(1)} %fusion.45, bf16[128,8,128]{0,2,1:T(8,128)(2,1)} %bitcast.311, bf16[1152,128]{1,0:T(8,128)(2,1)} %get-tuple-element.11), kind=kOutput, calls=%fused_computation.50 | convolution fusion | flops 306709632 | bytes 5427200 | tf_op jit(solution)/shard_map/sub | solution.py:77
  107.9 3.0 %fusion.40 = bf16[8,128,1152]{1,2,0:T(8,128)(2,1)S(1)} fusion(f32[8,128]{1,0:T(8,128)} %get-tuple-element.38, f32[8,128,1152]{1,2,0:T(8,128)} %get-tuple-element.39), kind=kLoop, calls=%fused_computation.77 | loop fusion | flops 2359296 | bytes 7081984 | tf_op jit(solution)/shard_map/convert_element_type | solution.py:79
  112.3 1.8 copy-done.20
  114.1 1.3 fusion.19
  115.4 1.5 fusion.31
  117.0 5.4 %exponential_reduce_fusion.2 = (f32[8,128]{1,0:T(8,128)}, f32[8,128,1152]{1,2,0:T(8,128)}) fusion(pred[128,1152]{0,1:T(8,128)(4,1)S(1)} %fusion.45, bf16[128,8,128]{0,2,1:T(8,128)(2,1)} %bitcast.309, bf16[1152,128]{1,0:T(8,128)(2,1)} %get-tuple-element.12), kind=kOutput, calls=%fused_computation.48 | convolution fusion | flops 306709632 | bytes 5427200 | tf_op jit(solution)/shard_map/sub | solution.py:77
  122.4 3.0 %fusion.41 = bf16[8,128,1152]{1,2,0:T(8,128)(2,1)S(1)} fusion(f32[8,128]{1,0:T(8,128)} %get-tuple-element.36, f32[8,128,1152]{1,2,0:T(8,128)} %get-tuple-element.37), kind=kLoop, calls=%fused_computation.78 | loop fusion | flops 2359296 | bytes 7081984 | tf_op jit(solution)/shard_map/convert_element_type | solution.py:79
  126.8 1.8 copy-done.21
  128.6 2.9 %fusion.16 = bf16[8,128,1152]{1,2,0:T(8,128)(2,1)} fusion(bf16[128,8,128]{0,2,1:T(8,128)(2,1)S(1)} %bitcast.296, f32[8,128]{1,0:T(8,128)S(1)} %bitcast.316, f32[8,128]{1,0:T(8,128)S(1)} %copy-done.50, f32[8,128,1152]{1,2,0:T(8,128)S(1)} %copy-done.21, bf16[1024,1024]{1,0:T(8,128)(2,1)S(1)} %bitcast.280, bf16[128,1024]{1,0:T(8,128)(2,1)S(1)} %bitcast_select_fusion.10), kind=kOutput, calls=%fused_computation.32 | convolution fusion | flops 308477952 | bytes 9707520 | tf_op jit(solution)/shard_map/tgd,ld->gtl/dot_general | solution.py:85
  131.5 5.4 %exponential_reduce_fusion.1 = (f32[8,128]{1,0:T(8,128)}, f32[8,128,1152]{1,2,0:T(8,128)}) fusion(pred[128,1152]{0,1:T(8,128)(4,1)S(1)} %fusion.45, bf16[128,8,128]{0,2,1:T(8,128)(2,1)} %bitcast.307, bf16[1152,128]{1,0:T(8,128)(2,1)} %get-tuple-element.13), kind=kOutput, calls=%fused_computation.46 | convolution fusion | flops 306709632 | bytes 5427200 | tf_op jit(solution)/shard_map/sub | solution.py:77
  136.9 3.2 %fusion.42 = bf16[8,128,1152]{1,2,0:T(8,128)(2,1)S(1)} fusion(f32[8,128]{1,0:T(8,128)} %get-tuple-element.34, f32[8,128,1152]{1,2,0:T(8,128)} %get-tuple-element.35), kind=kLoop, calls=%fused_computation.79 | loop fusion | flops 2359296 | bytes 7081984 | tf_op jit(solution)/shard_map/convert_element_type | solution.py:79
  141.6 1.8 copy-done.19
  143.4 1.3 fusion.13
  148.0 1.4 copy-done.15
  149.4 3.8 %exponential_reduce_fusion = (f32[8,128]{1,0:T(8,128)S(1)}, f32[8,128,1152]{1,2,0:T(8,128)}) fusion(pred[128,1152]{0,1:T(8,128)(4,1)S(1)} %fusion.45, bf16[128,8,128]{0,2,1:T(8,128)(2,1)S(1)} %bitcast.305, bf16[1152,128]{1,0:T(8,128)(2,1)S(1)} %copy-done.33), kind=kOutput, calls=%fused_computation.44 | convolution fusion | flops 306709632 | bytes 5427200 | tf_op jit(solution)/shard_map/sub | solution.py:77
  153.2 3.1 %fusion.43 = bf16[8,128,1152]{1,2,0:T(8,128)(2,1)S(1)} fusion(f32[8,128]{1,0:T(8,128)S(1)} %get-tuple-element.32, f32[8,128,1152]{1,2,0:T(8,128)} %get-tuple-element.33), kind=kLoop, calls=%fused_computation.80 | loop fusion | flops 2359296 | bytes 7081984 | tf_op jit(solution)/shard_map/convert_element_type | solution.py:79
  157.5 1.3 fusion.10
  160.6 1.1 copy-done.1
  166.8 1.6 slice.137
  168.9 11.5 %all-to-all-start.1 = ((bf16[32,32,1024]{2,1,0:T(8,128)(2,1)}), bf16[32,32,1024]{2,1,0:T(8,128)(2,1)}, u32[]{:S(2)}, u32[]{:S(2)}) async-start(bf16[32,32,1024]{2,1,0:T(8,128)(2,1)} %bitcast.283), calls=%async_computation.1 | async-start | bytes 4194304 | tf_op jit(solution)/shard_map/all_to_all | solution.py:36
  181.1 1.9 select_bitcast_fusion.2
  183.1 2.1 collective-permute-start.6
  185.2 1.5 convolution_convert_fusion.3
  190.1 1.4 collective-permute-start.5
  191.5 38.9 %all-to-all-done.1 = bf16[32,32,1024]{2,1,0:T(8,128)(2,1)} async-done(((bf16[32,32,1024]{2,1,0:T(8,128)(2,1)}), bf16[32,32,1024]{2,1,0:T(8,128)(2,1)}, u32[]{:S(2)}, u32[]{:S(2)}) %all-to-all-start.1) | async-done | bytes 2097184 | tf_op jit(solution)/shard_map/all_to_all | solution.py:36
  230.4 2.0 convert_reduce_fusion
  233.5 4.4 %all-to-all-start.2 = ((f32[8,32,1024]{2,1,0:T(8,128)}), f32[8,32,1024]{2,1,0:T(8,128)S(1)}, u32[]{:S(2)}, u32[]{:S(2)}) async-start(f32[8,32,1024]{2,1,0:T(8,128)} %broadcast_in_dim.54), calls=%async_computation.2 | async-start | bytes 2097152 | tf_op jit(solution)/shard_map/all_to_all | solution.py:42
  237.9 1.2 maximum_select_fusion
  240.3 2.7 %copy.150 = bf16[2,128,4096]{2,1,0:T(8,128)(2,1)} copy(bf16[2,128,4096]{1,2,0:T(8,128)(2,1)S(1)} %pad_maximum_fusion) | data formatting | bytes 4194304
  243.0 11.2 %all-to-all-done.2 = f32[8,32,1024]{2,1,0:T(8,128)S(1)} async-done(((f32[8,32,1024]{2,1,0:T(8,128)}), f32[8,32,1024]{2,1,0:T(8,128)S(1)}, u32[]{:S(2)}, u32[]{:S(2)}) %all-to-all-start.2) | async-done | bytes 1048608 | tf_op jit(solution)/shard_map/all_to_all | solution.py:42
  (138 shorter events, 26.4 us)
Async XLA Ops:
  1.9 94.1 %collective-permute-start.3 = (s32[1]{0:T(128)}, s32[1]{0:T(128)}, u32[]{:S(2)}, u32[]{:S(2)}) collective-permute-start(s32[1]{0:T(128)} %get-tuple-element.30), channel_id=1, source_target_pairs={{16,0},{17,1},{18,2},{19,3},{20,4},{21,5},{22,6},{23,7},{24,8},{25... | collective-permute-start | bytes 20 | tf_op jit(solution)/shard_map/ppermute | solution.py:25
  6.7 94.6 %all-to-all-start = ((bf16[32,32,1024]{2,1,0:T(8,128)(2,1)}), bf16[32,32,1024]{2,1,0:T(8,128)(2,1)S(1)}, u32[]{:S(2)}, u32[]{:S(2)}) async-start(bf16[32,32,1024]{2,1,0:T(8,128)(2,1)} %stack.12), calls=%async_computation | async-start | bytes 4194304 | tf_op jit(solution)/shard_map/all_to_all | solution.py:15
  22.1 75.3 %collective-permute-start.2 = (bf16[128,4096]{0,1:T(8,128)(2,1)}, bf16[128,4096]{0,1:T(8,128)(2,1)}, u32[]{:S(2)}, u32[]{:S(2)}) collective-permute-start(bf16[128,4096]{0,1:T(8,128)(2,1)} %bitcast.301), channel_id=1, source_target_pairs={{16,0},{17,1},{18,2},{19,3},{20,4},{21,5},{22,6},{23,7},{24,8},{25... | collective-permute-start | bytes 3145736 | tf_op jit(solution)/shard_map/ppermute | solution.py:25
  27.3 6.9 %copy-start.51 = (s32[2]{0:T(128)S(1)}, s32[2]{0:T(128)}, u32[]{:S(2)}) copy-start(s32[2]{0:T(128)} %param.11) | copy-start | bytes 28
  27.3 8.8 %copy-start.52 = (s32[2]{0:T(128)S(1)}, s32[2]{0:T(128)}, u32[]{:S(2)}) copy-start(s32[2]{0:T(128)} %param.10) | copy-start | bytes 28
  29.6 67.9 %collective-permute-start.4 = (bf16[128,4096]{0,1:T(8,128)(2,1)}, bf16[128,4096]{0,1:T(8,128)(2,1)}, u32[]{:S(2)}, u32[]{:S(2)}) collective-permute-start(bf16[128,4096]{0,1:T(8,128)(2,1)} %bitcast.302), channel_id=1, source_target_pairs={{16,0},{17,1},{18,2},{19,3},{20,4},{21,5},{22,6},{23,7},{24,8},{25... | collective-permute-start | bytes 3145736 | tf_op jit(solution)/shard_map/ppermute | solution.py:25
  32.0 65.4 %collective-permute-start = (bf16[128,1024]{1,0:T(8,128)(2,1)S(1)}, bf16[128,1024]{1,0:T(8,128)(2,1)}, u32[]{:S(2)}, u32[]{:S(2)}) collective-permute-start(bf16[128,1024]{1,0:T(8,128)(2,1)S(1)} %slice_bitcast_fusion), channel_id=1, source_target_pairs={{16,0},{17,1},{18,2},{19,3},{20,4},{21,5},{22,6},{23,7},{24,8},{25... | collective-permute-start | bytes 786440 | tf_op jit(solution)/shard_map/ppermute | solution.py:25
  34.7 59.0 %collective-permute-start.1 = (s32[1]{0:T(128)}, s32[1]{0:T(128)}, u32[]{:S(2)}, u32[]{:S(2)}) collective-permute-start(s32[1]{0:T(128)} %get-tuple-element.28), channel_id=1, source_target_pairs={{16,0},{17,1},{18,2},{19,3},{20,4},{21,5},{22,6},{23,7},{24,8},{25... | collective-permute-start | bytes 20 | tf_op jit(solution)/shard_map/ppermute | solution.py:25
  38.1 59.3 %copy-start.45 = (bf16[2,128,1024]{2,1,0:T(8,128)(2,1)S(1)}, bf16[2,128,1024]{2,1,0:T(8,128)(2,1)}, u32[]{:S(2)}) copy-start(bf16[2,128,1024]{2,1,0:T(8,128)(2,1)} %param.8) | copy-start | bytes 1572868
  107.9 3.0 %copy-start.31 = (bf16[128,1024]{0,1:T(8,128)(2,1)S(1)}, bf16[128,1024]{0,1:T(8,128)(2,1)}, u32[]{:S(2)}) copy-start(bf16[128,1024]{0,1:T(8,128)(2,1)} %get-tuple-element.24) | copy-start | bytes 786436
  110.9 3.2 %copy-start.20 = (f32[8,128,1152]{1,2,0:T(8,128)S(1)}, f32[8,128,1152]{1,2,0:T(8,128)}, u32[]{:S(2)}) copy-start(f32[8,128,1152]{1,2,0:T(8,128)} %get-tuple-element.39) | copy-start | bytes 14155780
  110.9 3.2 %copy-start.49 = (f32[8,128]{1,0:T(8,128)S(1)}, f32[8,128]{1,0:T(8,128)}, u32[]{:S(2)}) copy-start(f32[8,128]{1,0:T(8,128)} %get-tuple-element.38) | copy-start | bytes 12292
  122.4 3.0 %copy-start.29 = (bf16[128,1024]{0,1:T(8,128)(2,1)S(1)}, bf16[128,1024]{0,1:T(8,128)(2,1)}, u32[]{:S(2)}) copy-start(bf16[128,1024]{0,1:T(8,128)(2,1)} %get-tuple-element.27) | copy-start | bytes 786436
  125.4 3.2 %copy-start.21 = (f32[8,128,1152]{1,2,0:T(8,128)S(1)}, f32[8,128,1152]{1,2,0:T(8,128)}, u32[]{:S(2)}) copy-start(f32[8,128,1152]{1,2,0:T(8,128)} %get-tuple-element.37) | copy-start | bytes 14155780
  125.4 3.2 %copy-start.50 = (f32[8,128]{1,0:T(8,128)S(1)}, f32[8,128]{1,0:T(8,128)}, u32[]{:S(2)}) copy-start(f32[8,128]{1,0:T(8,128)} %get-tuple-element.36) | copy-start | bytes 12292
  136.9 3.3 %copy-start.27 = (bf16[128,1024]{0,1:T(8,128)(2,1)S(1)}, bf16[128,1024]{0,1:T(8,128)(2,1)}, u32[]{:S(2)}) copy-start(bf16[128,1024]{0,1:T(8,128)(2,1)} %get-tuple-element.26) | copy-start | bytes 786436
  140.2 3.2 %copy-start.19 = (f32[8,128,1152]{1,2,0:T(8,128)S(1)}, f32[8,128,1152]{1,2,0:T(8,128)}, u32[]{:S(2)}) copy-start(f32[8,128,1152]{1,2,0:T(8,128)} %get-tuple-element.35) | copy-start | bytes 14155780
  140.2 3.2 %copy-start.48 = (f32[8,128]{1,0:T(8,128)S(1)}, f32[8,128]{1,0:T(8,128)}, u32[]{:S(2)}) copy-start(f32[8,128]{1,0:T(8,128)} %get-tuple-element.34) | copy-start | bytes 12292
  143.4 1.7 copy-start.8
  143.4 2.4 copy-start.14
  143.4 2.4 copy-start.43
  147.1 2.3 copy-start.33
  147.1 2.3 copy-start.40
  153.2 3.1 %copy-start.46 = (f32[8,128]{1,0:T(8,128)}, f32[8,128]{1,0:T(8,128)S(1)}, u32[]{:S(2)}) copy-start(f32[8,128]{1,0:T(8,128)S(1)} %get-tuple-element.32) | copy-start | bytes 12292
  153.2 3.1 %copy-start.37 = (bf16[1152,128,1]{1,0,2:T(8,128)(2,1)S(1)}, bf16[1152,128,1]{1,0,2:T(8,128)(2,1)}, u32[]{:S(2)}) copy-start(bf16[1152,128,1]{1,0,2:T(8,128)(2,1)} %get-tuple-element.14) | copy-start | bytes 884740
  153.2 3.9 %copy-start.18 = (f32[8,128,1152]{1,2,0:T(8,128)S(1)}, f32[8,128,1152]{1,2,0:T(8,128)}, u32[]{:S(2)}) copy-start(f32[8,128,1152]{1,2,0:T(8,128)} %get-tuple-element.33) | copy-start | bytes 14155780
  157.5 1.7 copy-start.41
  159.2 2.5 copy-start.1
  159.2 2.5 copy-start.32
  161.7 1.7 copy-start.30
  163.3 1.7 copy-start.28
  166.8 2.1 copy-start.17
  168.9 16.3 %copy-start.7 = (bf16[8,128,1152]{1,2,0:T(8,128)(2,1)S(1)}, bf16[8,128,1152]{1,2,0:T(8,128)(2,1)}, u32[]{:S(2)}) copy-start(bf16[8,128,1152]{1,2,0:T(8,128)(2,1)} %copy-done.6) | copy-start | bytes 7077892
  168.9 61.5 %all-to-all-start.1 = ((bf16[32,32,1024]{2,1,0:T(8,128)(2,1)}), bf16[32,32,1024]{2,1,0:T(8,128)(2,1)}, u32[]{:S(2)}, u32[]{:S(2)}) async-start(bf16[32,32,1024]{2,1,0:T(8,128)(2,1)} %bitcast.283), calls=%async_computation.1 | async-start | bytes 4194304 | tf_op jit(solution)/shard_map/all_to_all | solution.py:36
  180.4 6.3 %copy-start.36 = (bf16[1152,128]{1,0:T(8,128)(2,1)S(1)}, bf16[1152,128]{1,0:T(8,128)(2,1)}, u32[]{:S(2)}) copy-start(bf16[1152,128]{1,0:T(8,128)(2,1)} %get-tuple-element.12) | copy-start | bytes 884740
  181.1 5.6 %copy-start.9 = (bf16[8,128,1152]{1,2,0:T(8,128)(2,1)S(1)}, bf16[8,128,1152]{1,2,0:T(8,128)(2,1)}, u32[]{:S(2)}) copy-start(bf16[8,128,1152]{1,2,0:T(8,128)(2,1)} %fusion.16) | copy-start | bytes 7077892
  183.1 4.2 %copy-start.11 = (bf16[8,128,1152]{1,2,0:T(8,128)(2,1)S(1)}, bf16[8,128,1152]{1,2,0:T(8,128)(2,1)}, u32[]{:S(2)}) copy-start(bf16[8,128,1152]{1,2,0:T(8,128)(2,1)} %copy-done.10) | copy-start | bytes 7077892
  183.1 4.2 %copy-start.35 = (bf16[1152,128]{1,0:T(8,128)(2,1)S(1)}, bf16[1152,128]{1,0:T(8,128)(2,1)}, u32[]{:S(2)}) copy-start(bf16[1152,128]{1,0:T(8,128)(2,1)} %get-tuple-element.13) | copy-start | bytes 884740
  183.1 56.0 %collective-permute-start.6 = (bf16[128,1024]{1,0:T(8,128)(2,1)}, bf16[128,1024]{1,0:T(8,128)(2,1)}, u32[]{:S(2)}, u32[]{:S(2)}) collective-permute-start(bf16[128,1024]{1,0:T(8,128)(2,1)} %get-tuple-element.10), channel_id=1, source_target_pairs={{16,0},{17,1},{18,2},{19,3},{20,4},{21,5},{22,6},{23,7},{24,8},{25... | collective-permute-start | bytes 786440 | tf_op jit(solution)/shard_map/ppermute | solution.py:25
  186.7 1.8 copy-start.13
  186.7 1.8 copy-start.34
  187.3 1.7 copy-start.22
  189.0 44.4 %copy-start.26 = (bf16[128,8,128]{2,0,1:T(8,128)(2,1)}, bf16[128,8,128]{2,0,1:T(8,128)(2,1)S(1)}, u32[]{:S(2)}) copy-start(bf16[128,8,128]{2,0,1:T(8,128)(2,1)S(1)} %convolution_convert_fusion) | copy-start | bytes 786436
  190.1 47.8 %copy-start.23 = (bf16[128,8,128]{2,0,1:T(8,128)(2,1)S(1)}, bf16[128,8,128]{2,0,1:T(8,128)(2,1)}, u32[]{:S(2)}) copy-start(bf16[128,8,128]{2,0,1:T(8,128)(2,1)} %copy-done.22) | copy-start | bytes 786436
  190.1 49.9 %collective-permute-start.5 = (bf16[128,4096]{0,1:T(8,128)(2,1)}, bf16[128,4096]{0,1:T(8,128)(2,1)S(1)}, u32[]{:S(2)}, u32[]{:S(2)}) collective-permute-start(bf16[128,4096]{0,1:T(8,128)(2,1)} %pad_maximum_fusion.1), channel_id=1, source_target_pairs={{16,0},{17,1},{18,2},{19,3},{20,4},{21,5},{22,6},{23,7},{24,8},{25... | collective-permute-start | bytes 3145736 | tf_op jit(solution)/shard_map/ppermute | solution.py:25
  191.5 46.4 %copy-start.25 = (bf16[128,8,128]{2,0,1:T(8,128)(2,1)S(1)}, bf16[128,8,128]{2,0,1:T(8,128)(2,1)}, u32[]{:S(2)}) copy-start(bf16[128,8,128]{2,0,1:T(8,128)(2,1)} %copy-done.24) | copy-start | bytes 786436
  233.5 5.7 %copy-start.38 = (bf16[1,128,1024]{2,1,0:T(8,128)(2,1)S(1)}, bf16[1,128,1024]{2,1,0:T(8,128)(2,1)}, u32[]{:S(2)}) copy-start(bf16[1,128,1024]{2,1,0:T(8,128)(2,1)} %get-tuple-element.9) | copy-start | bytes 786436
  233.5 20.8 %all-to-all-start.2 = ((f32[8,32,1024]{2,1,0:T(8,128)}), f32[8,32,1024]{2,1,0:T(8,128)S(1)}, u32[]{:S(2)}, u32[]{:S(2)}) async-start(f32[8,32,1024]{2,1,0:T(8,128)} %broadcast_in_dim.54), calls=%async_computation.2 | async-start | bytes 2097152 | tf_op jit(solution)/shard_map/all_to_all | solution.py:42
  (15 other events, 21.6 us)
